TPU v7x, 32 devices: a whole 2x2x4 slice. The times are simulated.
32 devices in a mesh: frames: 4 (over y, x), rows: 8 (over z, core).
Axes of the slice: x: 2, y: 2, z: 4, core: 2. Of those that a mesh axis runs over, the one named last changes fastest.
Arguments:
- inputs: bfloat16 [4, 32, 424, 256], P('frames', 'rows'), may hold values from -350 to 350, as said below
- cotangent: bfloat16 [4, 32, 424, 256], P('frames', 'rows'), may hold values from -140 to 140, as said below
- kernel: bfloat16 [3, 3, 3, 256, 256], replicated, may hold values from -0.078125 to 0.078125
- norm_gain: float32 [256], replicated, may hold values from 0.1 to 1.9
- norm_bias: float32 [256], replicated, may hold values from -1 to 1
Outputs:
- input_grad: bfloat16 [4, 32, 424, 256], P('frames', 'rows')
Inputs may be any that keep to these rules, and one draw needn't show every extreme that they name: `inputs`: finite values. `cotangent`: finite values.
All inputs are finite; a program needn't handle non-finite values.
Results may differ from a plain program's by a relative error of at most 0.0055.
Values may be sent and summed in bfloat16 or wider, within the bound.
No kernel may reach another device: no remote copies, remote signals or barrier semaphores. Data moves between devices by JAX's collectives and lax.ppermute only.
A program may use at most 64 MiB of HBM per device.

v0:
```python
import jax
import jax.numpy as jnp
from jax import lax
from jax.sharding import PartitionSpec as P

GROUPS = 32
EPS = 1e-06


def from_behind(value, axis, by):
    devices = lax.axis_size(axis)
    pairs = [(i, i + by) for i in range(devices) if 0 <= i + by < devices]
    return lax.ppermute(value, axis, pairs)


def padded_2(value, sides, width):
    for axis, dim in sides:
        devices, length = (lax.axis_size(axis), value.shape[dim])
        up = [(i, (i + 1) % devices) for i in range(devices - 1)]
        down = [(j, i) for i, j in up]
        last = lax.slice_in_dim(value, length - width, length, axis=dim)
        first = lax.slice_in_dim(value, 0, width, axis=dim)
        before = lax.ppermute(last, axis, up)
        after = lax.ppermute(first, axis, down)
        value = jnp.concatenate([before, value, after], axis=dim)
    return value


def group_sum(values):
    per_chan = jnp.sum(values, axis=(0, 1))
    return jnp.sum(per_chan.reshape(GROUPS, -1), axis=1)


def spread_groups(per_group, channels):
    return jnp.repeat(per_group, channels // GROUPS)


def transpose_conv(rimmed, flipped, strip, width, channels):
    padded = jnp.pad(rimmed, ((0, 0), (0, 0), (1, 1), (0, 0)))
    act_grad = jnp.zeros((strip, width, channels), jnp.float32)
    for row_tap in range(3):
        for col_tap in range(3):
            window = padded[
                :, 2 - row_tap : 2 - row_tap + strip, 2 - col_tap : 2 - col_tap + width, :
            ]
            act_grad = act_grad + jnp.einsum(
                "myxo,mco->yxc",
                window,
                flipped[:, row_tap, col_tap],
                preferred_element_type=jnp.float32,
            )
    return act_grad


def shards(inputs, cotangent, kernel, norm_gain, norm_bias):
    values = inputs[0].astype(jnp.float32)
    strip, width, channels = values.shape
    cells_per = (
        lax.axis_size("frames") * lax.axis_size("rows") * strip * width * (channels // GROUPS)
    )
    flipped = kernel[::-1]
    own_slab = cotangent[0]
    later = from_behind(own_slab, "frames", -1)
    latest = from_behind(own_slab, "frames", -2)
    stacked = jnp.stack([own_slab, later, latest])
    rimmed = padded_2(stacked, (("rows", 1),), 1)
    act_grad = transpose_conv(rimmed, flipped, strip, width, channels)
    totals, squares = lax.psum((group_sum(values), group_sum(values * values)), ("frames", "rows"))
    centre = totals / cells_per
    variance = jnp.maximum(squares / cells_per - centre * centre, 0.0)
    centred = values - spread_groups(centre, channels)
    inv_std = spread_groups(lax.rsqrt(variance + EPS), channels)
    normed = centred * inv_std
    preact = normed * norm_gain + norm_bias
    logistic = jax.nn.sigmoid(preact)
    norm_grad = act_grad * logistic * (1.0 + preact * (1.0 - logistic)) * norm_gain
    grad_total, grad_cross = lax.psum(
        (group_sum(norm_grad), group_sum(norm_grad * normed)), ("frames", "rows")
    )
    grad_total = grad_total / cells_per
    grad_cross = grad_cross / cells_per
    input_grad = inv_std * (
        norm_grad
        - spread_groups(grad_total, channels)
        - normed * spread_groups(grad_cross, channels)
    )
    return input_grad.astype(jnp.bfloat16)[None]


def solution(mesh):
    return jax.shard_map(
        shards,
        mesh=mesh,
        in_specs=(P("frames", "rows", None, None), P("frames", "rows", None, None), P(), P(), P()),
        out_specs=P("frames", "rows", None, None),
        check_vma=False,
    )
```

profile of v0, /device:TPU:14, one launch (start us, length us, event | category | flops | bytes accessed | tf_op | source)
XLA Modules:
  0.0 156.6 jit_solution(9935320973470033081)
XLA Ops:
  0.0 3.3 %collective-permute-start.1 = (bf16[4,424,256]{2,1,0:T(8,128)(2,1)}, bf16[4,424,256]{2,1,0:T(8,128)(2,1)}, u32[]{:S(2)}, u32[]{:S(2)}) collective-permute-start(bf16[4,424,256]{2,1,0:T(8,128)(2,1)} %bitcast.146), channel_id=1, source_target_pairs={{16,0},{24,8},{17,1},{25,9},{18,2},{26,10},{19,3},{27,11},{20,4},{... | collective-permute-start | bytes 2605064 | tf_op jit(solution)/shard_map/ppermute | solution.py:13
  3.3 3.4 %collective-permute-start = (bf16[4,424,256]{2,1,0:T(8,128)(2,1)}, bf16[4,424,256]{2,1,0:T(8,128)(2,1)}, u32[]{:S(2)}, u32[]{:S(2)}) collective-permute-start(bf16[4,424,256]{2,1,0:T(8,128)(2,1)} %bitcast.147), channel_id=1, source_target_pairs={{8,0},{16,8},{24,16},{9,1},{17,9},{25,17},{10,2},{18,10},{26,18},{... | collective-permute-start | bytes 2605064 | tf_op jit(solution)/shard_map/ppermute | solution.py:13
  6.7 2.0 %fusion.42 = f32[256]{0:T(256)} fusion(bf16[1,4,424,256]{3,2,1,0:T(8,128)(2,1)} %param.5), kind=kLoop, calls=%fused_computation.48 | loop fusion | flops 1302272 | bytes 869376 | tf_op jit(solution)/shard_map/reduce_sum | solution.py:30
  8.7 0.9 reshape.19
  9.6 2.2 %convert_reduce_fusion = f32[256]{0:T(256)} fusion(bf16[1,4,424,256]{3,2,1,0:T(8,128)(2,1)} %param.5), kind=kLoop, calls=%fused_computation.44 | loop fusion | flops 868096 | bytes 869376 | tf_op jit(solution)/shard_map/reduce_sum | solution.py:30
  11.7 1.4 reshape.20
  13.1 0.7 reduce_sum.73
  13.8 0.8 reduce_sum.75
  14.6 59.9 %all-reduce.2 = (f32[32]{0:T(128)S(1)}, f32[32]{0:T(128)S(1)}) all-reduce(f32[32]{0:T(128)S(1)} %reduce_sum.75, f32[32]{0:T(128)} %reduce_sum.73), channel_id=1, replica_groups=mesh['frames'=4,'rows'=8] {'frames','rows'}, use_global_device_ids=true, to_apply=%region_5.6 | all-reduce | flops 64 | bytes 512 | tf_op jit(solution)/shard_map/psum | solution.py:68
  75.8 0.7 broadcast_in_dim.19
  76.5 0.6 sub.30
  77.1 2.6 %pad_maximum_fusion = (bf16[3,1,424,256]{3,2,0,1:T(8,128)(2,1)}, bf16[3,1,424,256]{3,2,0,1:T(8,128)(2,1)}) fusion(bf16[1,4,424,256]{3,2,0,1:T(8,128)(2,1)} %bitcast.5, bf16[1,4,424,256]{3,2,0,1:T(8,128)(2,1)} %bitcast.4, bf16[1,4,424,256]{3,2,0,1:T(8,128)(2,1)} %bitcast.148), kind=kLoop, calls=%fused_computation.76 | loop fusion | flops 1302528 | bytes 3907584 | tf_op jit(solution)/shard_map/slice | solution.py:22
  79.7 2.7 %collective-permute-start.3 = (bf16[3,1,424,256]{3,2,0,1:T(8,128)(2,1)}, bf16[3,1,424,256]{3,2,0,1:T(8,128)(2,1)}, u32[]{:S(2)}, u32[]{:S(2)}) collective-permute-start(bf16[3,1,424,256]{3,2,0,1:T(8,128)(2,1)} %get-tuple-element.20), channel_id=1, source_target_pairs={{1,0},{2,1},{3,2},{4,3},{5,4},{6,5},{7,6},{9,8},{10,9},{11,10},{12... | collective-permute-start | bytes 1953800 | tf_op jit(solution)/shard_map/ppermute | solution.py:24
  82.4 1.9 %collective-permute-start.2 = (bf16[3,1,424,256]{3,2,0,1:T(8,128)(2,1)}, bf16[3,1,424,256]{3,2,0,1:T(8,128)(2,1)}, u32[]{:S(2)}, u32[]{:S(2)}) collective-permute-start(bf16[3,1,424,256]{3,2,0,1:T(8,128)(2,1)} %get-tuple-element.21), channel_id=1, source_target_pairs={{0,1},{1,2},{2,3},{3,4},{4,5},{5,6},{6,7},{8,9},{9,10},{10,11},{11... | collective-permute-start | bytes 1953800 | tf_op jit(solution)/shard_map/ppermute | solution.py:23
  84.3 1.9 %fusion.77 = (bf16[3,1,1,256,256]{4,3,2,1,0:T(8,128)(2,1)}, bf16[3,1,1,256,256]{4,3,2,1,0:T(8,128)(2,1)}, bf16[3,1,1,256,256]{4,3,2,1,0:T(8,128)(2,1)}, bf16[3,1...) fusion(bf16[3,3,3,256,256]{4,3,2,1,0:T(8,128)(2,1)S(1)} %copy-d, ...), kind=kLoop, calls=%fused_computation.95 | loop fusion | bytes 7077888 | tf_op jit(solution)/shard_map/slice | solution.py:49
  86.2 1.9 %slice.117 = bf16[3,1,1,256,256]{4,3,2,1,0:T(8,128)(2,1)} reverse(bf16[3,1,1,256,256]{4,3,2,1,0:T(8,128)(2,1)} %get-tuple-element.11), dimensions={0} | reverse | bytes 786432 | tf_op jit(solution)/shard_map/slice | solution.py:49
  88.1 1.8 %slice.111 = bf16[3,1,1,256,256]{4,3,2,1,0:T(8,128)(2,1)} reverse(bf16[3,1,1,256,256]{4,3,2,1,0:T(8,128)(2,1)} %get-tuple-element.12), dimensions={0} | reverse | bytes 786432 | tf_op jit(solution)/shard_map/slice | solution.py:49
  89.9 1.8 %slice.108 = bf16[3,1,1,256,256]{4,3,2,1,0:T(8,128)(2,1)} reverse(bf16[3,1,1,256,256]{4,3,2,1,0:T(8,128)(2,1)} %get-tuple-element.13), dimensions={0} | reverse | bytes 786432 | tf_op jit(solution)/shard_map/slice | solution.py:49
  91.8 0.8 slice.105
  92.8 0.8 slice.114
  93.6 2.4 %fusion.34 = f32[4,424,256,1]{2,1,3,0:T(8,128)S(1)} fusion(bf16[1,4,424,256]{3,2,0,1:T(8,128)(2,1)} %bitcast.5, bf16[1,4,424,256]{3,2,0,1:T(8,128)(2,1)} %bitcast.4, bf16[1,4,424,256]{3,2,0,1:T(8,128)(2,1)S(1)} %bitcast.149, bf16[3,1,1,256,256]{4,3,2,1,0:T(8,128)(2,1)} %slice.105), kind=kOutput, calls=%fused_computation.38 | convolution fusion | flops 669499392 | bytes 4734976 | tf_op jit(solution)/shard_map/myxo,mco->yxc/dot_general | solution.py:46
  96.0 4.5 %select_maximum_fusion = bf16[3,6,426,256]{3,2,0,1:T(8,128)(2,1)S(1)} fusion(bf16[3,1,424,256]{3,2,0,1:T(8,128)(2,1)} %collective-permute-done.3, bf16[3,1,424,256]{3,2,0,1:T(8,128)(2,1)} %collective-permute-done.2, bf16[1,4,424,256]{3,2,0,1:T(8,128)(2,1)} %bitcast.5, bf16[1,4,424,256]{3,2,0,1:T(8,128)(2,1)} %bitcast.4, bf16[1,4,424,256]{3,2,0,1:T(8,128)(2,1)S(1)} %bitcast.150), kind=kLoop, calls=%fused_computation.3 | loop fusion | flops 35334144 | bytes 7833600 | tf_op jit(solution)/shard_map/concatenate | solution.py:25
  100.5 1.0 fusion.24
  101.5 0.9 fusion.26
  102.5 1.0 fusion.28
  103.4 0.9 fusion.30
  104.4 1.0 fusion.32
  105.4 2.4 %fusion.14 = f32[4,424,256,1]{2,1,3,0:T(8,128)S(1)} fusion(bf16[1,4,424,256]{3,2,0,1:T(8,128)(2,1)} %bitcast.5, bf16[1,4,424,256]{3,2,0,1:T(8,128)(2,1)} %bitcast.4, bf16[1,4,424,256]{3,2,0,1:T(8,128)(2,1)S(1)} %bitcast.151, bf16[3,1,424,256]{3,2,0,1:T(8,128)(2,1)} %collective-permute-done.2, bf16[3,1,1,256,256]{4,3,2,1,0:T(8,128)(2,1)S(1)} %copy-done.12), kind=kOutput, calls=%fused_computation.18 | convolution fusion | flops 679919616 | bytes 5386240 | tf_op jit(solution)/shard_map/myxo,mco->yxc/dot_general | solution.py:46
  107.8 2.5 %fusion.6 = f32[4,424,256,1]{2,1,3,0:T(8,128)S(1)} fusion(bf16[3,1,424,256]{3,2,0,1:T(8,128)(2,1)} %collective-permute-done.3, bf16[1,4,424,256]{3,2,0,1:T(8,128)(2,1)} %bitcast.5, bf16[1,4,424,256]{3,2,0,1:T(8,128)(2,1)} %bitcast.4, bf16[1,4,424,256]{3,2,0,1:T(8,128)(2,1)S(1)} %bitcast.152, bf16[3,1,1,256,256]{4,3,2,1,0:T(8,128)(2,1)S(1)} %slice.97), kind=kOutput, calls=%fused_computation.10 | convolution fusion | flops 679919616 | bytes 5386240 | tf_op jit(solution)/shard_map/myxo,mco->yxc/dot_general | solution.py:46
  110.3 2.1 %fusion.76 = (f32[256]{0:T(256)S(1)}, f32[256]{0:T(256)S(1)}, f32[4,424,256]{2,1,0:T(8,128)S(1)}) fusion(f32[256]{0:T(256)S(1)} %copy-done.13, f32[256]{0:T(256)S(1)} %copy-done.14, bf16[1,4,424,256]{3,2,1,0:T(8,128)(2,1)S(1)} %copy-done, f32[256]{0:T(256)S(1)} %copy-done.15, f32[256]{0:T(256)S(1)} %copy-done.16, ...), kind=kOutput, calls=%fused_computation.94 | convolution fusion | flops 677748224 | bytes 19503104 | tf_op jit(solution)/shard_map/myxo,mco->yxc/dot_general | solution.py:46
  112.9 42.1 %all-reduce.1 = (f32[32]{0:T(128)S(1)}, f32[32]{0:T(128)S(1)}) all-reduce(f32[32]{0:T(128)S(1)} %reduce_sum.79, f32[32]{0:T(128)S(1)} %reduce_sum.77), channel_id=1, replica_groups=mesh['frames'=4,'rows'=8] {'frames','rows'}, use_global_device_ids=true, to_apply=%region_11.12 | all-reduce | flops 64 | bytes 512 | tf_op jit(solution)/shard_map/psum | solution.py:77
  155.3 1.3 fusion.63
  (54 shorter events, 2.2 us)
Async XLA Ops:
  0.0 77.1 %collective-permute-start.1 = (bf16[4,424,256]{2,1,0:T(8,128)(2,1)}, bf16[4,424,256]{2,1,0:T(8,128)(2,1)}, u32[]{:S(2)}, u32[]{:S(2)}) collective-permute-start(bf16[4,424,256]{2,1,0:T(8,128)(2,1)} %bitcast.146), channel_id=1, source_target_pairs={{16,0},{24,8},{17,1},{25,9},{18,2},{26,10},{19,3},{27,11},{20,4},{... | collective-permute-start | bytes 2605064 | tf_op jit(solution)/shard_map/ppermute | solution.py:13
  3.3 73.8 %collective-permute-start = (bf16[4,424,256]{2,1,0:T(8,128)(2,1)}, bf16[4,424,256]{2,1,0:T(8,128)(2,1)}, u32[]{:S(2)}, u32[]{:S(2)}) collective-permute-start(bf16[4,424,256]{2,1,0:T(8,128)(2,1)} %bitcast.147), channel_id=1, source_target_pairs={{8,0},{16,8},{24,16},{9,1},{17,9},{25,17},{10,2},{18,10},{26,18},{... | collective-permute-start | bytes 2605064 | tf_op jit(solution)/shard_map/ppermute | solution.py:13
  8.7 75.7 %copy-start.1 = (bf16[3,3,3,256,256]{4,3,2,1,0:T(8,128)(2,1)S(1)}, bf16[3,3,3,256,256]{4,3,2,1,0:T(8,128)(2,1)}, u32[]{:S(2)}) copy-start(bf16[3,3,3,256,256]{4,3,2,1,0:T(8,128)(2,1)} %param.7) | copy-start | bytes 10616836
  79.7 16.3 %collective-permute-start.3 = (bf16[3,1,424,256]{3,2,0,1:T(8,128)(2,1)}, bf16[3,1,424,256]{3,2,0,1:T(8,128)(2,1)}, u32[]{:S(2)}, u32[]{:S(2)}) collective-permute-start(bf16[3,1,424,256]{3,2,0,1:T(8,128)(2,1)} %get-tuple-element.20), channel_id=1, source_target_pairs={{1,0},{2,1},{3,2},{4,3},{5,4},{6,5},{7,6},{9,8},{10,9},{11,10},{12... | collective-permute-start | bytes 1953800 | tf_op jit(solution)/shard_map/ppermute | solution.py:24
  82.4 13.6 %collective-permute-start.2 = (bf16[3,1,424,256]{3,2,0,1:T(8,128)(2,1)}, bf16[3,1,424,256]{3,2,0,1:T(8,128)(2,1)}, u32[]{:S(2)}, u32[]{:S(2)}) collective-permute-start(bf16[3,1,424,256]{3,2,0,1:T(8,128)(2,1)} %get-tuple-element.21), channel_id=1, source_target_pairs={{0,1},{1,2},{2,3},{3,4},{4,5},{5,6},{6,7},{8,9},{9,10},{10,11},{11... | collective-permute-start | bytes 1953800 | tf_op jit(solution)/shard_map/ppermute | solution.py:23
  86.2 5.6 %copy-start.8 = (bf16[3,1,1,256,256]{4,3,2,1,0:T(8,128)(2,1)S(1)}, bf16[3,1,1,256,256]{4,3,2,1,0:T(8,128)(2,1)}, u32[]{:S(2)}) copy-start(bf16[3,1,1,256,256]{4,3,2,1,0:T(8,128)(2,1)} %get-tuple-element.14) | copy-start | bytes 1179652
  86.2 6.4 %copy-start.7 = (bf16[3,1,1,256,256]{4,3,2,1,0:T(8,128)(2,1)S(1)}, bf16[3,1,1,256,256]{4,3,2,1,0:T(8,128)(2,1)}, u32[]{:S(2)}) copy-start(bf16[3,1,1,256,256]{4,3,2,1,0:T(8,128)(2,1)} %get-tuple-element.15) | copy-start | bytes 1179652
  86.2 6.4 %copy-start.6 = (bf16[3,1,1,256,256]{4,3,2,1,0:T(8,128)(2,1)S(1)}, bf16[3,1,1,256,256]{4,3,2,1,0:T(8,128)(2,1)}, u32[]{:S(2)}) copy-start(bf16[3,1,1,256,256]{4,3,2,1,0:T(8,128)(2,1)} %get-tuple-element.16) | copy-start | bytes 1179652
  86.2 6.5 %copy-start.5 = (bf16[3,1,1,256,256]{4,3,2,1,0:T(8,128)(2,1)S(1)}, bf16[3,1,1,256,256]{4,3,2,1,0:T(8,128)(2,1)}, u32[]{:S(2)}) copy-start(bf16[3,1,1,256,256]{4,3,2,1,0:T(8,128)(2,1)} %get-tuple-element.17) | copy-start | bytes 1179652
  86.2 6.5 %copy-start.4 = (bf16[3,1,1,256,256]{4,3,2,1,0:T(8,128)(2,1)S(1)}, bf16[3,1,1,256,256]{4,3,2,1,0:T(8,128)(2,1)}, u32[]{:S(2)}) copy-start(bf16[3,1,1,256,256]{4,3,2,1,0:T(8,128)(2,1)} %get-tuple-element.18) | copy-start | bytes 1179652
  88.1 4.6 %copy-start.3 = (bf16[3,1,1,256,256]{4,3,2,1,0:T(8,128)(2,1)S(1)}, bf16[3,1,1,256,256]{4,3,2,1,0:T(8,128)(2,1)}, u32[]{:S(2)}) copy-start(bf16[3,1,1,256,256]{4,3,2,1,0:T(8,128)(2,1)} %get-tuple-element.19) | copy-start | bytes 1179652
  89.9 3.6 %copy-start.2 = (bf16[1,4,424,256]{3,2,1,0:T(8,128)(2,1)S(1)}, bf16[1,4,424,256]{3,2,1,0:T(8,128)(2,1)}, u32[]{:S(2)}) copy-start(bf16[1,4,424,256]{3,2,1,0:T(8,128)(2,1)} %param.6) | copy-start | bytes 2605060
  96.0 4.5 %copy-start.10 = (bf16[3,1,1,256,256]{4,3,2,1,0:T(8,128)(2,1)S(1)}, bf16[3,1,1,256,256]{4,3,2,1,0:T(8,128)(2,1)}, u32[]{:S(2)}) copy-start(bf16[3,1,1,256,256]{4,3,2,1,0:T(8,128)(2,1)} %slice.111) | copy-start | bytes 1179652
  100.5 1.0 copy-start.11
  104.4 1.0 copy-start.12
  107.7 2.5 %copy-start = (bf16[1,4,424,256]{3,2,1,0:T(8,128)(2,1)S(1)}, bf16[1,4,424,256]{3,2,1,0:T(8,128)(2,1)}, u32[]{:S(2)}) copy-start(bf16[1,4,424,256]{3,2,1,0:T(8,128)(2,1)} %param.5) | copy-start | bytes 2605060
  107.8 2.5 %copy-start.9 = (bf16[3,1,1,256,256]{4,3,2,1,0:T(8,128)(2,1)S(1)}, bf16[3,1,1,256,256]{4,3,2,1,0:T(8,128)(2,1)}, u32[]{:S(2)}) copy-start(bf16[3,1,1,256,256]{4,3,2,1,0:T(8,128)(2,1)} %slice.117) | copy-start | bytes 1179652
  107.8 2.5 %copy-start.13 = (f32[256]{0:T(256)S(1)}, f32[256]{0:T(256)}, u32[]{:S(2)}) copy-start(f32[256]{0:T(256)} %mul.60) | copy-start | bytes 3076
  107.8 2.5 %copy-start.14 = (f32[256]{0:T(256)S(1)}, f32[256]{0:T(256)}, u32[]{:S(2)}) copy-start(f32[256]{0:T(256)} %sub.30) | copy-start | bytes 3076
  107.8 2.5 %copy-start.15 = (f32[256]{0:T(256)S(1)}, f32[256]{0:T(256)}, u32[]{:S(2)}) copy-start(f32[256]{0:T(256)} %param.9) | copy-start | bytes 3076
  107.8 2.5 %copy-start.16 = (f32[256]{0:T(256)S(1)}, f32[256]{0:T(256)}, u32[]{:S(2)}) copy-start(f32[256]{0:T(256)} %param.8) | copy-start | bytes 3076
where the time goes:
time: 157 us
  blocking collectives  102 us (65%)
  other arithmetic  14.9 us (9%)
  matrix products  14.1 us (9%)
  local copies, waits for them, and re-layouts  14 us (9%)
  starting transfers between devices  11.3 us (7%)
    psum x1, blocking collectives, shards(): lax.psum((group_sum(values), group_sum(values * values)), ('frames', 'row...  59.9 us
    psum x1, blocking collectives, shards(): lax.psum((group_sum(norm_grad), group_sum(norm_grad * normed)), ('frames'...  42.1 us
    dot_general x9, matrix products, transpose_conv(): jnp.einsum('myxo,mco->yxc', window, flipped[:, row_tap, col_tap], preferr...  14.1 us
    slice x10, local copies, waits for them, and re-layouts, transpose_conv(): flipped[:, row_tap, col_tap]  9.11 us
    ppermute x2, starting transfers between devices, from_behind(): return lax.ppermute(value, axis, pairs)  6.69 us
    concatenate x1, other arithmetic, padded_2(): value = jnp.concatenate([before, value, after], axis=dim)  4.5 us
    reduce_sum x2, other arithmetic, group_sum(): per_chan = jnp.sum(values, axis=(0, 1))  4.14 us
  transfers between devices with their start and end apart: 4, of which 0 were waited for; matrix products, arithmetic and copies ran while one was open for 14% of the time, Pallas kernels for 0%

commit v1 on v0

--- a/solution.py
+++ b/solution.py
@@ -75,7 +75,7 @@
     logistic = jax.nn.sigmoid(preact)
     norm_grad = act_grad * logistic * (1.0 + preact * (1.0 - logistic)) * norm_gain
     grad_total, grad_cross = lax.psum(
-        (group_sum(norm_grad), group_sum(norm_grad * normed)), ("frames", "rows")
+        lax.psum((group_sum(norm_grad), group_sum(norm_grad * normed)), "rows"), "frames"
     )
     grad_total = grad_total / cells_per
     grad_cross = grad_cross / cells_per

time: 157 us -> 143 us (0.911)
  the two profiles are of different devices: /device:TPU:14 before, /device:TPU:0 now
where the time goes in v1:
time: 143 us; the launch traced here: 142 us
  blocking collectives  91.2 us (64%)
  other arithmetic  14.9 us (10%)
  matrix products  14.1 us (10%)
  local copies, waits for them, and re-layouts  14 us (10%)
  starting transfers between devices  7.73 us (5%)
    psum x1, blocking collectives, shards(): lax.psum((group_sum(values), group_sum(values * values)), ('frames', 'row...  67.4 us
    psum x1, blocking collectives, shards(): lax.psum((group_sum(norm_grad), group_sum(norm_grad * normed)), 'rows')  14.1 us
    dot_general x9, matrix products, transpose_conv(): jnp.einsum('myxo,mco->yxc', window, flipped[:, row_tap, col_tap], preferr...  14.1 us
    psum x1, blocking collectives, shards(): lax.psum(lax.psum((group_sum(norm_grad), group_sum(norm_grad * normed)),...  9.74 us
    slice x10, local copies, waits for them, and re-layouts, transpose_conv(): flipped[:, row_tap, col_tap]  9.11 us
    concatenate x1, other arithmetic, padded_2(): value = jnp.concatenate([before, value, after], axis=dim)  4.5 us
    reduce_sum x2, other arithmetic, group_sum(): per_chan = jnp.sum(values, axis=(0, 1))  4.14 us
    ppermute x1, starting transfers between devices, padded_2(): before = lax.ppermute(last, axis, up)  3.87 us
  transfers between devices with their start and end apart: 4, of which 0 were waited for; matrix products, arithmetic and copies ran while one was open for 15% of the time, Pallas kernels for 0%

profile of v1, /device:TPU:0, one launch (start us, length us, event | category | flops | bytes accessed | tf_op | source)
XLA Modules:
  0.0 142.3 jit_solution(3402151632776045116)
XLA Ops:
  0.0 1.3 collective-permute-start.1
  1.3 1.3 collective-permute-start
  2.6 2.0 %fusion.42 = f32[256]{0:T(256)} fusion(bf16[1,4,424,256]{3,2,1,0:T(8,128)(2,1)} %param.5), kind=kLoop, calls=%fused_computation.48 | loop fusion | flops 1302272 | bytes 869376 | tf_op jit(solution)/shard_map/reduce_sum | solution.py:30
  4.6 0.9 reshape.19
  5.5 2.2 %convert_reduce_fusion = f32[256]{0:T(256)} fusion(bf16[1,4,424,256]{3,2,1,0:T(8,128)(2,1)} %param.5), kind=kLoop, calls=%fused_computation.44 | loop fusion | flops 868096 | bytes 869376 | tf_op jit(solution)/shard_map/reduce_sum | solution.py:30
  7.6 1.4 reshape.20
  9.0 0.7 reduce_sum.73
  9.7 0.8 reduce_sum.75
  10.5 67.4 %all-reduce.1 = (f32[32]{0:T(128)S(1)}, f32[32]{0:T(128)S(1)}) all-reduce(f32[32]{0:T(128)S(1)} %reduce_sum.75, f32[32]{0:T(128)} %reduce_sum.73), channel_id=1, replica_groups=mesh['frames'=4,'rows'=8] {'frames','rows'}, use_global_device_ids=true, to_apply=%region_5.6 | all-reduce | flops 64 | bytes 512 | tf_op jit(solution)/shard_map/psum | solution.py:68
  79.1 0.7 broadcast_in_dim.19
  80.5 2.6 %pad_maximum_fusion = (bf16[3,1,424,256]{3,2,0,1:T(8,128)(2,1)}, bf16[3,1,424,256]{3,2,0,1:T(8,128)(2,1)}) fusion(bf16[1,4,424,256]{3,2,0,1:T(8,128)(2,1)} %bitcast.5, bf16[1,4,424,256]{3,2,0,1:T(8,128)(2,1)} %bitcast.4, bf16[1,4,424,256]{3,2,0,1:T(8,128)(2,1)} %bitcast.148), kind=kLoop, calls=%fused_computation.76 | loop fusion | flops 1302528 | bytes 3907584 | tf_op jit(solution)/shard_map/slice | solution.py:22
  83.1 1.3 collective-permute-start.3
  84.4 3.9 %collective-permute-start.2 = (bf16[3,1,424,256]{3,2,0,1:T(8,128)(2,1)}, bf16[3,1,424,256]{3,2,0,1:T(8,128)(2,1)}, u32[]{:S(2)}, u32[]{:S(2)}) collective-permute-start(bf16[3,1,424,256]{3,2,0,1:T(8,128)(2,1)} %get-tuple-element.23), channel_id=1, source_target_pairs={{0,1},{1,2},{2,3},{3,4},{4,5},{5,6},{6,7},{8,9},{9,10},{10,11},{11... | collective-permute-start | bytes 1953800 | tf_op jit(solution)/shard_map/ppermute | solution.py:23
  88.2 1.9 %fusion.77 = (bf16[3,1,1,256,256]{4,3,2,1,0:T(8,128)(2,1)}, bf16[3,1,1,256,256]{4,3,2,1,0:T(8,128)(2,1)}, bf16[3,1,1,256,256]{4,3,2,1,0:T(8,128)(2,1)}, bf16[3,1...) fusion(bf16[3,3,3,256,256]{4,3,2,1,0:T(8,128)(2,1)S(1)} %copy-d, ...), kind=kLoop, calls=%fused_computation.95 | loop fusion | bytes 7077888 | tf_op jit(solution)/shard_map/slice | solution.py:49
  90.1 1.9 %slice.117 = bf16[3,1,1,256,256]{4,3,2,1,0:T(8,128)(2,1)} reverse(bf16[3,1,1,256,256]{4,3,2,1,0:T(8,128)(2,1)} %get-tuple-element.13), dimensions={0} | reverse | bytes 786432 | tf_op jit(solution)/shard_map/slice | solution.py:49
  92.0 1.8 %slice.111 = bf16[3,1,1,256,256]{4,3,2,1,0:T(8,128)(2,1)} reverse(bf16[3,1,1,256,256]{4,3,2,1,0:T(8,128)(2,1)} %get-tuple-element.14), dimensions={0} | reverse | bytes 786432 | tf_op jit(solution)/shard_map/slice | solution.py:49
  93.8 1.8 %slice.108 = bf16[3,1,1,256,256]{4,3,2,1,0:T(8,128)(2,1)} reverse(bf16[3,1,1,256,256]{4,3,2,1,0:T(8,128)(2,1)} %get-tuple-element.15), dimensions={0} | reverse | bytes 786432 | tf_op jit(solution)/shard_map/slice | solution.py:49
  95.7 0.8 slice.105
  96.7 0.8 slice.114
  97.4 2.4 %fusion.34 = f32[4,424,256,1]{2,1,3,0:T(8,128)S(1)} fusion(bf16[1,4,424,256]{3,2,0,1:T(8,128)(2,1)} %bitcast.5, bf16[1,4,424,256]{3,2,0,1:T(8,128)(2,1)} %bitcast.4, bf16[1,4,424,256]{3,2,0,1:T(8,128)(2,1)S(1)} %bitcast.149, bf16[3,1,1,256,256]{4,3,2,1,0:T(8,128)(2,1)} %slice.105), kind=kOutput, calls=%fused_computation.38 | convolution fusion | flops 669499392 | bytes 4734976 | tf_op jit(solution)/shard_map/myxo,mco->yxc/dot_general | solution.py:46
  99.9 4.5 %select_maximum_fusion = bf16[3,6,426,256]{3,2,0,1:T(8,128)(2,1)S(1)} fusion(bf16[3,1,424,256]{3,2,0,1:T(8,128)(2,1)} %collective-permute-done.3, bf16[3,1,424,256]{3,2,0,1:T(8,128)(2,1)} %collective-permute-done.2, bf16[1,4,424,256]{3,2,0,1:T(8,128)(2,1)} %bitcast.5, bf16[1,4,424,256]{3,2,0,1:T(8,128)(2,1)} %bitcast.4, bf16[1,4,424,256]{3,2,0,1:T(8,128)(2,1)S(1)} %bitcast.150), kind=kLoop, calls=%fused_computation.3 | loop fusion | flops 35334144 | bytes 7833600 | tf_op jit(solution)/shard_map/concatenate | solution.py:25
  104.4 1.0 fusion.24
  105.4 0.9 fusion.26
  106.4 1.0 fusion.28
  107.3 0.9 fusion.30
  108.3 1.0 fusion.32
  109.3 2.4 %fusion.14 = f32[4,424,256,1]{2,1,3,0:T(8,128)S(1)} fusion(bf16[1,4,424,256]{3,2,0,1:T(8,128)(2,1)} %bitcast.5, bf16[1,4,424,256]{3,2,0,1:T(8,128)(2,1)} %bitcast.4, bf16[1,4,424,256]{3,2,0,1:T(8,128)(2,1)S(1)} %bitcast.151, bf16[3,1,424,256]{3,2,0,1:T(8,128)(2,1)} %collective-permute-done.2, bf16[3,1,1,256,256]{4,3,2,1,0:T(8,128)(2,1)S(1)} %copy-done.12), kind=kOutput, calls=%fused_computation.18 | convolution fusion | flops 679919616 | bytes 5386240 | tf_op jit(solution)/shard_map/myxo,mco->yxc/dot_general | solution.py:46
  111.7 2.5 %fusion.6 = f32[4,424,256,1]{2,1,3,0:T(8,128)S(1)} fusion(bf16[3,1,424,256]{3,2,0,1:T(8,128)(2,1)} %collective-permute-done.3, bf16[1,4,424,256]{3,2,0,1:T(8,128)(2,1)} %bitcast.5, bf16[1,4,424,256]{3,2,0,1:T(8,128)(2,1)} %bitcast.4, bf16[1,4,424,256]{3,2,0,1:T(8,128)(2,1)S(1)} %bitcast.152, bf16[3,1,1,256,256]{4,3,2,1,0:T(8,128)(2,1)S(1)} %slice.97), kind=kOutput, calls=%fused_computation.10 | convolution fusion | flops 679919616 | bytes 5386240 | tf_op jit(solution)/shard_map/myxo,mco->yxc/dot_general | solution.py:46
  114.2 2.1 %fusion.76 = (f32[256]{0:T(256)S(1)}, f32[256]{0:T(256)S(1)}, f32[4,424,256]{2,1,0:T(8,128)S(1)}) fusion(f32[256]{0:T(256)S(1)} %copy-done.13, f32[256]{0:T(256)S(1)} %copy-done.14, bf16[1,4,424,256]{3,2,1,0:T(8,128)(2,1)S(1)} %copy-done, f32[256]{0:T(256)S(1)} %copy-done.15, f32[256]{0:T(256)S(1)} %copy-done.16, ...), kind=kOutput, calls=%fused_computation.94 | convolution fusion | flops 677748224 | bytes 19503104 | tf_op jit(solution)/shard_map/myxo,mco->yxc/dot_general | solution.py:46
  116.7 14.1 %all-reduce.2 = (f32[32]{0:T(128)S(1)}, f32[32]{0:T(128)S(1)}) all-reduce(f32[32]{0:T(128)S(1)} %reduce_sum.79, f32[32]{0:T(128)S(1)} %reduce_sum.77), channel_id=1, replica_groups=mesh['frames'=4,'rows'=8] {'rows'}, use_global_device_ids=true, to_apply=%region_12.13 | all-reduce | flops 64 | bytes 512 | tf_op jit(solution)/shard_map/psum | solution.py:78
  130.9 9.7 %all-reduce.3 = (f32[32]{0:T(128)S(1)}, f32[32]{0:T(128)S(1)}) all-reduce(f32[32]{0:T(128)S(1)} %get-tuple-element.9, f32[32]{0:T(128)S(1)} %get-tuple-element.10), channel_id=1, replica_groups=mesh['frames'=4,'rows'=8] {'frames'}, use_global_device_ids=true, to_apply=%region_13.14 | all-reduce | flops 64 | bytes 512 | tf_op jit(solution)/shard_map/psum | solution.py:77
  140.9 1.3 fusion.63
  (55 shorter events, 2.8 us)
Async XLA Ops:
  0.0 80.5 %collective-permute-start.1 = (bf16[4,424,256]{2,1,0:T(8,128)(2,1)}, bf16[4,424,256]{2,1,0:T(8,128)(2,1)}, u32[]{:S(2)}, u32[]{:S(2)}) collective-permute-start(bf16[4,424,256]{2,1,0:T(8,128)(2,1)} %bitcast.146), channel_id=1, source_target_pairs={{16,0},{24,8},{17,1},{25,9},{18,2},{26,10},{19,3},{27,11},{20,4},{... | collective-permute-start | bytes 2605064 | tf_op jit(solution)/shard_map/ppermute | solution.py:13
  1.3 79.2 %collective-permute-start = (bf16[4,424,256]{2,1,0:T(8,128)(2,1)}, bf16[4,424,256]{2,1,0:T(8,128)(2,1)}, u32[]{:S(2)}, u32[]{:S(2)}) collective-permute-start(bf16[4,424,256]{2,1,0:T(8,128)(2,1)} %bitcast.147), channel_id=1, source_target_pairs={{8,0},{16,8},{24,16},{9,1},{17,9},{25,17},{10,2},{18,10},{26,18},{... | collective-permute-start | bytes 2605064 | tf_op jit(solution)/shard_map/ppermute | solution.py:13
  4.6 83.7 %copy-start.1 = (bf16[3,3,3,256,256]{4,3,2,1,0:T(8,128)(2,1)S(1)}, bf16[3,3,3,256,256]{4,3,2,1,0:T(8,128)(2,1)}, u32[]{:S(2)}) copy-start(bf16[3,3,3,256,256]{4,3,2,1,0:T(8,128)(2,1)} %param.7) | copy-start | bytes 10616836
  83.1 16.8 %collective-permute-start.3 = (bf16[3,1,424,256]{3,2,0,1:T(8,128)(2,1)}, bf16[3,1,424,256]{3,2,0,1:T(8,128)(2,1)}, u32[]{:S(2)}, u32[]{:S(2)}) collective-permute-start(bf16[3,1,424,256]{3,2,0,1:T(8,128)(2,1)} %get-tuple-element.22), channel_id=1, source_target_pairs={{1,0},{2,1},{3,2},{4,3},{5,4},{6,5},{7,6},{9,8},{10,9},{11,10},{12... | collective-permute-start | bytes 1953800 | tf_op jit(solution)/shard_map/ppermute | solution.py:24
  84.4 15.5 %collective-permute-start.2 = (bf16[3,1,424,256]{3,2,0,1:T(8,128)(2,1)}, bf16[3,1,424,256]{3,2,0,1:T(8,128)(2,1)}, u32[]{:S(2)}, u32[]{:S(2)}) collective-permute-start(bf16[3,1,424,256]{3,2,0,1:T(8,128)(2,1)} %get-tuple-element.23), channel_id=1, source_target_pairs={{0,1},{1,2},{2,3},{3,4},{4,5},{5,6},{6,7},{8,9},{9,10},{10,11},{11... | collective-permute-start | bytes 1953800 | tf_op jit(solution)/shard_map/ppermute | solution.py:23
  90.1 5.6 %copy-start.8 = (bf16[3,1,1,256,256]{4,3,2,1,0:T(8,128)(2,1)S(1)}, bf16[3,1,1,256,256]{4,3,2,1,0:T(8,128)(2,1)}, u32[]{:S(2)}) copy-start(bf16[3,1,1,256,256]{4,3,2,1,0:T(8,128)(2,1)} %get-tuple-element.16) | copy-start | bytes 1179652
  90.1 6.4 %copy-start.7 = (bf16[3,1,1,256,256]{4,3,2,1,0:T(8,128)(2,1)S(1)}, bf16[3,1,1,256,256]{4,3,2,1,0:T(8,128)(2,1)}, u32[]{:S(2)}) copy-start(bf16[3,1,1,256,256]{4,3,2,1,0:T(8,128)(2,1)} %get-tuple-element.17) | copy-start | bytes 1179652
  90.1 6.4 %copy-start.6 = (bf16[3,1,1,256,256]{4,3,2,1,0:T(8,128)(2,1)S(1)}, bf16[3,1,1,256,256]{4,3,2,1,0:T(8,128)(2,1)}, u32[]{:S(2)}) copy-start(bf16[3,1,1,256,256]{4,3,2,1,0:T(8,128)(2,1)} %get-tuple-element.18) | copy-start | bytes 1179652
  90.1 6.5 %copy-start.5 = (bf16[3,1,1,256,256]{4,3,2,1,0:T(8,128)(2,1)S(1)}, bf16[3,1,1,256,256]{4,3,2,1,0:T(8,128)(2,1)}, u32[]{:S(2)}) copy-start(bf16[3,1,1,256,256]{4,3,2,1,0:T(8,128)(2,1)} %get-tuple-element.19) | copy-start | bytes 1179652
  90.1 6.5 %copy-start.4 = (bf16[3,1,1,256,256]{4,3,2,1,0:T(8,128)(2,1)S(1)}, bf16[3,1,1,256,256]{4,3,2,1,0:T(8,128)(2,1)}, u32[]{:S(2)}) copy-start(bf16[3,1,1,256,256]{4,3,2,1,0:T(8,128)(2,1)} %get-tuple-element.20) | copy-start | bytes 1179652
  92.0 4.6 %copy-start.3 = (bf16[3,1,1,256,256]{4,3,2,1,0:T(8,128)(2,1)S(1)}, bf16[3,1,1,256,256]{4,3,2,1,0:T(8,128)(2,1)}, u32[]{:S(2)}) copy-start(bf16[3,1,1,256,256]{4,3,2,1,0:T(8,128)(2,1)} %get-tuple-element.21) | copy-start | bytes 1179652
  93.8 3.6 %copy-start.2 = (bf16[1,4,424,256]{3,2,1,0:T(8,128)(2,1)S(1)}, bf16[1,4,424,256]{3,2,1,0:T(8,128)(2,1)}, u32[]{:S(2)}) copy-start(bf16[1,4,424,256]{3,2,1,0:T(8,128)(2,1)} %param.6) | copy-start | bytes 2605060
  99.9 4.5 %copy-start.10 = (bf16[3,1,1,256,256]{4,3,2,1,0:T(8,128)(2,1)S(1)}, bf16[3,1,1,256,256]{4,3,2,1,0:T(8,128)(2,1)}, u32[]{:S(2)}) copy-start(bf16[3,1,1,256,256]{4,3,2,1,0:T(8,128)(2,1)} %slice.111) | copy-start | bytes 1179652
  104.4 1.0 copy-start.11
  108.3 1.0 copy-start.12
  111.6 2.5 %copy-start = (bf16[1,4,424,256]{3,2,1,0:T(8,128)(2,1)S(1)}, bf16[1,4,424,256]{3,2,1,0:T(8,128)(2,1)}, u32[]{:S(2)}) copy-start(bf16[1,4,424,256]{3,2,1,0:T(8,128)(2,1)} %param.5) | copy-start | bytes 2605060
  111.6 2.5 %copy-start.9 = (bf16[3,1,1,256,256]{4,3,2,1,0:T(8,128)(2,1)S(1)}, bf16[3,1,1,256,256]{4,3,2,1,0:T(8,128)(2,1)}, u32[]{:S(2)}) copy-start(bf16[3,1,1,256,256]{4,3,2,1,0:T(8,128)(2,1)} %slice.117) | copy-start | bytes 1179652
  111.7 2.5 %copy-start.13 = (f32[256]{0:T(256)S(1)}, f32[256]{0:T(256)}, u32[]{:S(2)}) copy-start(f32[256]{0:T(256)} %mul.60) | copy-start | bytes 3076
  111.7 2.5 %copy-start.14 = (f32[256]{0:T(256)S(1)}, f32[256]{0:T(256)}, u32[]{:S(2)}) copy-start(f32[256]{0:T(256)} %sub.30) | copy-start | bytes 3076
  111.7 2.5 %copy-start.15 = (f32[256]{0:T(256)S(1)}, f32[256]{0:T(256)}, u32[]{:S(2)}) copy-start(f32[256]{0:T(256)} %param.9) | copy-start | bytes 3076
  111.7 2.5 %copy-start.16 = (f32[256]{0:T(256)S(1)}, f32[256]{0:T(256)}, u32[]{:S(2)}) copy-start(f32[256]{0:T(256)} %param.8) | copy-start | bytes 3076
